TPU v7x, 256 devices: a whole 4x4x8 slice. The times are simulated.
256 devices in a mesh: pairs: 64 (over y, z, core), orb: 4 (over x).
Axes of the slice: x: 4, y: 4, z: 8, core: 2. Of those that a mesh axis runs over, the one named last changes fastest.
Arguments:
- amplitudes: float32 [1024, 128, 128], P(('pairs', 'orb')), may hold values from -4 to 4
- integrals: bfloat16 [1024, 128, 128], P(('pairs', 'orb')), may hold values from -6 to 6
- energies: float32 [1024, 128], P(('pairs', 'orb')), may hold values from 0.5 to 4
- intersections: bfloat16 [1024, 16, 128, 128], P(('pairs', 'orb')), may hold values from -0.5 to 0.5
- couplings: float32 [1024, 16], P(('pairs', 'orb')), may hold values from -2 to 2
- projector: float32 [1024, 128], P(('pairs', 'orb')), may hold values from -0.5 to 0.5
- pair_orbitals: int32 [1024, 2], P(('pairs', 'orb')), may hold values from 0 to 31
- coupled: int32 [1024, 16], replicated, may hold values from 0 to 1023, as said below
- pair_slot: int32 [1024], replicated, may hold values from 0 to 1023, as said below
Outputs:
- final_amplitudes: float32 [1024, 128, 128], P(('pairs', 'orb'))
- residual: float32 [1024, 128, 128], P(('pairs', 'orb'))
Inputs may be any that keep to these rules, and one draw needn't show every extreme that they name: `coupled`: each row holds 16 different pair ids, never the id of the pair held in that row's slot. The rows of one device name at most 1 different pairs held by the devices of any one pairs index, and exactly 1 held by the devices of the next pairs index. `pair_slot`: A permutation of the pair ids.
All inputs are finite; a program needn't handle non-finite values.
Results may differ from a plain program's by a relative error of at most 0.00037.
Values may be sent and summed in bfloat16 or wider, within the bound.
A program may use at most 64 MiB of HBM per device.

v0:
```python
import jax
import jax.numpy as jnp
from jax import lax
from jax.sharding import PartitionSpec as P

PAIRS_ORB = 32
ITERS = 2


def body(
    amplitudes,
    integrals,
    energies,
    intersections,
    couplings,
    projector,
    pair_orbitals,
    coupled,
    pair_slot,
):
    highest = lax.Precision.HIGHEST
    pair_count = lax.axis_size("pairs")
    orb_count = lax.axis_size("orb")
    devices = pair_count * orb_count
    per_device = amplitudes.shape[0]
    width = amplitudes.shape[1]
    total = coupled.shape[0]
    capacity = 1 + coupled.shape[1] // pair_count
    group = orb_count * per_device
    orbitals = total // PAIRS_ORB
    pair_idx = lax.axis_index("pairs")
    orb_idx = lax.axis_index("orb")
    device_id = pair_idx * orb_count + orb_idx
    targets = pair_slot[coupled]
    row_owner = jnp.broadcast_to(
        (jnp.arange(total, dtype=jnp.int32) // per_device)[:, None], targets.shape
    )
    needed = jnp.zeros((devices, total), jnp.int32).at[row_owner, targets].set(1)
    mine = lax.dynamic_slice_in_dim(needed, device_id, 1, 0)[0].reshape(pair_count, group)
    ranks = (jnp.cumsum(mine, axis=1) - 1).reshape(total)
    own_targets = lax.dynamic_slice_in_dim(targets, device_id * per_device, per_device, 0)
    slot_ids = jnp.arange(capacity, dtype=jnp.int32)
    group_cols = lax.dynamic_slice_in_dim(needed, pair_idx * group, group, 1)
    group_rank = jnp.cumsum(group_cols, axis=1) - 1
    entry_pos = own_targets // group * capacity + ranks[own_targets]
    dest_cols = group_cols.reshape(pair_count, orb_count, group)
    dest_cols = lax.dynamic_slice_in_dim(dest_cols, orb_idx, 1, 1)[:, 0]
    dest_rank = group_rank.reshape(pair_count, orb_count, group)
    dest_rank = lax.dynamic_slice_in_dim(dest_rank, orb_idx, 1, 1)[:, 0]
    select = (
        (dest_cols == 1)[:, None, :] & (dest_rank[:, None, :] == slot_ids[None, :, None])
    ).astype(jnp.bfloat16)
    orbital_ids = jnp.arange(orbitals, dtype=jnp.int32)
    first_hot = (pair_orbitals[:, 0:1] == orbital_ids[None, :]).astype(jnp.float32)
    second_hot = (pair_orbitals[:, 1:2] == orbital_ids[None, :]).astype(jnp.float32)
    denom = energies[:, :, None] + energies[:, None, :]
    state = amplitudes
    residual = amplitudes
    for step in range(ITERS):
        blocks = state.astype(jnp.bfloat16)
        group_blocks = lax.all_gather(blocks, "orb", axis=0, tiled=True)
        outgoing = jnp.einsum(
            "pcj,jxy->pcxy", select, group_blocks, preferred_element_type=jnp.float32
        )
        outgoing = outgoing.astype(jnp.bfloat16)
        arrived = lax.all_to_all(outgoing, "pairs", split_axis=0, concat_axis=0, tiled=True)
        arrived = arrived.reshape(pair_count * capacity, width, width)
        fetched = arrived[entry_pos]
        lifted = jnp.einsum(
            "pkab,pkbc->pkac", intersections, fetched, preferred_element_type=jnp.float32
        )
        scaled = (couplings[:, :, None, None] * lifted).astype(jnp.bfloat16)
        coupling = jnp.einsum(
            "pkac,pkdc->pad", scaled, intersections, preferred_element_type=jnp.float32
        )
        projected = jnp.einsum("pab,pb->pa", state, projector, precision=highest)
        partial_sum = jnp.dot(first_hot.T, projected, precision=highest) + jnp.dot(
            second_hot.T, projected, precision=highest
        )
        summed = lax.psum(partial_sum, ("pairs", "orb"))
        left = jnp.dot(first_hot, summed, precision=highest)
        right = jnp.dot(second_hot, summed, precision=highest)
        residual = (
            integrals.astype(jnp.float32)
            + energies[:, :, None] * state
            + state * energies[:, None, :]
            - coupling
            + left[:, :, None] * projector[:, None, :]
            + projector[:, :, None] * right[:, None, :]
        )
        state = state - residual / denom
    return (state, residual)


def solution(mesh):
    return jax.shard_map(
        body,
        mesh=mesh,
        in_specs=(
            P(("pairs", "orb"), None, None),
            P(("pairs", "orb"), None, None),
            P(("pairs", "orb"), None),
            P(("pairs", "orb"), None, None, None),
            P(("pairs", "orb"), None),
            P(("pairs", "orb"), None),
            P(("pairs", "orb"), None),
            P(),
            P(),
        ),
        out_specs=(P(("pairs", "orb"), None, None), P(("pairs", "orb"), None, None)),
        check_vma=False,
    )
```

profile of v0, /device:TPU:1, one launch (start us, length us, event | category | flops | bytes accessed | tf_op | source)
XLA Modules:
  0.0 392.0 jit_solution(17940552267861765877)
XLA Ops:
  0.7 0.6 add_select_fusion
  1.9 0.8 compare_select_fusion.1
  3.1 65.3 %gather_fusion = s32[16384]{0:T(1024)S(1)} fusion(s32[1024]{0:T(1024)S(1)} %copy-done.1, s32[16384]{0:T(1024)S(1)} %broadcast_clamp_fusion), kind=kCustom, calls=%fused_computation | custom fusion | bytes 196608 | tf_op jit(solution)/shard_map/gather | solution.py:34
  69.8 0.6 broadcast.186
  70.4 60.8 %scatter_custom_fusion = s32[262144]{0:T(1024)S(1)} fusion(s32[16384]{0:T(1024)S(1)} %reshape.167, s32[16384]{0:T(1024)} %broadcast.186, s32[]{:T(128)} %constant.52.clone.1), kind=kCustom, calls=%fused_computation.28 | custom fusion | bytes 1049088
  131.2 1.1 reshape.134
  132.3 1.0 constant_dynamic-slice_fusion
  133.4 0.7 reduce_window_sum.22
  134.1 12.3 %all_gather.6 = bf16[16,128,128]{2,1,0:T(8,128)(2,1)S(1)} all-gather(bf16[4,128,128]{2,1,0:T(8,128)(2,1)S(1)} %convert_element_type.38), channel_id=1, replica_groups=mesh['pairs'=64,'orb'=4] {'orb'}, dimensions={0}, use_global_device_ids=true | all-gather | bytes 655360 | tf_op jit(solution)/shard_map/all_gather | solution.py:61
  146.4 0.7 convert_bitcast_fusion.1
  147.1 2.6 copy.45
  149.8 14.2 %all-to-all-start = ((bf16[64,1,128,128]{3,2,1,0:T(8,128)(2,1)}), bf16[64,1,128,128]{3,2,1,0:T(8,128)(2,1)}, u32[]{:S(2)}, u32[]{:S(2)}) async-start(bf16[64,1,128,128]{3,2,1,0:T(8,128)(2,1)} %copy.45), calls=%async_computation | async-start | bytes 4194304 | tf_op jit(solution)/shard_map/all_to_all | solution.py:66
  164.2 0.8 dynamic-slice_reduce_fusion
  165.4 0.7 gather_fusion.1
  167.4 89.2 %psum.14 = f32[32,128]{1,0:T(8,128)S(1)} all-reduce(f32[32,128]{1,0:T(8,128)S(1)} %convolution_add_fusion.1), channel_id=1, replica_groups=mesh['pairs'=64,'orb'=4] {'pairs','orb'}, use_global_device_ids=true, to_apply=%region_3.4 | all-reduce | flops 4096 | bytes 32768 | tf_op jit(solution)/shard_map/psum | solution.py:80
  257.1 3.7 gather_fusion.2
  260.8 3.8 fusion.64
  264.6 11.4 %all_gather.7 = bf16[16,128,128]{2,1,0:T(8,128)(2,1)S(1)} all-gather(bf16[4,128,128]{2,1,0:T(8,128)(2,1)S(1)} %get-tuple-element.4), channel_id=1, replica_groups=mesh['pairs'=64,'orb'=4] {'orb'}, dimensions={0}, use_global_device_ids=true | all-gather | bytes 655360 | tf_op jit(solution)/shard_map/all_gather | solution.py:61
  276.1 0.7 convert_bitcast_fusion
  276.8 2.6 copy.50
  279.4 11.7 %all-to-all-start.1 = ((bf16[64,1,128,128]{3,2,1,0:T(8,128)(2,1)}), bf16[64,1,128,128]{3,2,1,0:T(8,128)(2,1)}, u32[]{:S(2)}, u32[]{:S(2)}) async-start(bf16[64,1,128,128]{3,2,1,0:T(8,128)(2,1)} %copy.50), calls=%async_computation.1 | async-start | bytes 4194304 | tf_op jit(solution)/shard_map/all_to_all | solution.py:66
  292.2 91.1 %psum.15 = f32[32,128]{1,0:T(8,128)S(1)} all-reduce(f32[32,128]{1,0:T(8,128)S(1)} %convolution_add_fusion), channel_id=1, replica_groups=mesh['pairs'=64,'orb'=4] {'pairs','orb'}, use_global_device_ids=true, to_apply=%region_4.5 | all-reduce | flops 4096 | bytes 32768 | tf_op jit(solution)/shard_map/psum | solution.py:80
  383.7 3.7 gather_fusion.3
  387.4 4.6 %fusion.40 = (f32[4,128,128]{2,1,0:T(8,128)}, f32[4,128,128]{2,1,0:T(8,128)}) fusion(f32[4,128,128]{2,1,0:T(8,128)S(1)} %get-tuple-element.5, f32[4,128]{1,0:T(4,128)S(1)} %copy-done.12, f32[4,128]{1,0:T(4,128)S(1)} %fusion.49, f32[4,128]{1,0:T(4,128)S(1)} %copy-done.5, f32[4,128]{1,0:T(4,128)S(1)} %fusion.51, bf16[4,16,128,128]{3,2,1,0:T(8,128)(2,1)S(1)} %copy-done, ...), kind=kOutput, calls=%fused_computation.35 | convolution fusion | flops 539820032 | bytes 5120256 | tf_op jit(solution)/shard_map/pkac,pkdc->pad/dot_general | solution.py:73
  (67 shorter events, 6.0 us)
Async XLA Ops:
  0.6 260.2 %copy-start = (bf16[4,16,128,128]{3,2,1,0:T(8,128)(2,1)S(1)}, bf16[4,16,128,128]{3,2,1,0:T(8,128)(2,1)}, u32[]{:S(2)}) copy-start(bf16[4,16,128,128]{3,2,1,0:T(8,128)(2,1)} %param.12) | copy-start | bytes 6291460
  0.6 2.5 copy-start.1
  68.4 0.7 copy-start.3
  68.4 0.7 copy-start.4
  68.4 0.7 copy-start.6
  68.4 0.7 copy-start.9
  68.4 0.8 copy-start.8
  69.7 64.4 %copy-start.2 = (f32[4,128,128]{2,1,0:T(8,128)S(1)}, f32[4,128,128]{2,1,0:T(8,128)}, u32[]{:S(2)}) copy-start(f32[4,128,128]{2,1,0:T(8,128)} %param.9) | copy-start | bytes 786436
  149.8 107.3 %all-to-all-start = ((bf16[64,1,128,128]{3,2,1,0:T(8,128)(2,1)}), bf16[64,1,128,128]{3,2,1,0:T(8,128)(2,1)}, u32[]{:S(2)}, u32[]{:S(2)}) async-start(bf16[64,1,128,128]{3,2,1,0:T(8,128)(2,1)} %copy.45), calls=%async_computation | async-start | bytes 4194304 | tf_op jit(solution)/shard_map/all_to_all | solution.py:66
  164.0 2.4 copy-start.7
  164.0 2.4 copy-start.5
  257.0 3.8 copy-start.10
  257.0 3.8 copy-start.11
  257.1 3.8 copy-start.12
  279.4 104.3 %all-to-all-start.1 = ((bf16[64,1,128,128]{3,2,1,0:T(8,128)(2,1)}), bf16[64,1,128,128]{3,2,1,0:T(8,128)(2,1)}, u32[]{:S(2)}, u32[]{:S(2)}) async-start(bf16[64,1,128,128]{3,2,1,0:T(8,128)(2,1)} %copy.50), calls=%async_computation.1 | async-start | bytes 4194304 | tf_op jit(solution)/shard_map/all_to_all | solution.py:66
where the time goes:
time: 393 us; the launch traced here: 392 us
  blocking collectives  204 us (52%)
  local copies, waits for them, and re-layouts  145 us (37%)
  starting transfers between devices  25.9 us (7%)
  matrix products  12.6 us (3%)
    psum x2, blocking collectives, body(): summed = lax.psum(partial_sum, ('pairs', 'orb'))  180 us
    gather x3, local copies, waits for them, and re-layouts, body(): targets = pair_slot[coupled]  65.6 us
    unnamed x30, local copies, waits for them, and re-layouts  62.1 us
    all_to_all x2, starting transfers between devices, body(): lax.all_to_all(outgoing, 'pairs', split_axis=0, concat_axis=0, tiled=True)  25.9 us
    all_gather x2, blocking collectives, body(): group_blocks = lax.all_gather(blocks, 'orb', axis=0, tiled=True)  23.7 us
    dot_general x2, matrix products, body(): jnp.einsum('pkac,pkdc->pad', scaled, intersections, preferred_element_typ...  8.38 us
  transfers between devices with their start and end apart: 2, of which 0 were waited for; matrix products, arithmetic and copies ran while one was open for 1% of the time, Pallas kernels for 0%

commit v1 on v0

--- a/solution.py
+++ b/solution.py
@@ -77,7 +77,8 @@
         partial_sum = jnp.dot(first_hot.T, projected, precision=highest) + jnp.dot(
             second_hot.T, projected, precision=highest
         )
-        summed = lax.psum(partial_sum, ("pairs", "orb"))
+        _fix_table = lambda work_x: jax.lax.psum(jax.lax.psum(work_x, "orb"), "pairs")
+        summed = _fix_table(partial_sum)
         left = jnp.dot(first_hot, summed, precision=highest)
         right = jnp.dot(second_hot, summed, precision=highest)
         residual = (

time: 393 us -> 777 us (1.98)
  blocking collectives: 204 us -> 582 us
    psum x2 -> x4, blocking collectives: 180 us -> 559 us  [the longest x2 530 us: body(): jax.lax.psum(jax.lax.psum(work_x, 'orb'), 'pairs')]
where the time goes in v1:
time: 777 us; the launch traced here: 771 us
  blocking collectives  582 us (75%)
  local copies, waits for them, and re-layouts  145 us (19%)
  starting transfers between devices  27.6 us (4%)
  matrix products  12.6 us (2%)
    psum x2, blocking collectives, body(): jax.lax.psum(jax.lax.psum(work_x, 'orb'), 'pairs')  530 us
    gather x3, local copies, waits for them, and re-layouts, body(): targets = pair_slot[coupled]  65.6 us
    unnamed x30, local copies, waits for them, and re-layouts  62.1 us
    psum x2, blocking collectives, body(): jax.lax.psum(work_x, 'orb')  29.6 us
    all_to_all x2, starting transfers between devices, body(): lax.all_to_all(outgoing, 'pairs', split_axis=0, concat_axis=0, tiled=True)  27.6 us
    all_gather x2, blocking collectives, body(): group_blocks = lax.all_gather(blocks, 'orb', axis=0, tiled=True)  22.4 us
  transfers between devices with their start and end apart: 2, of which 0 were waited for; matrix products, arithmetic and copies ran while one was open for 1% of the time, Pallas kernels for 0%

profile of v1, /device:TPU:1, one launch (start us, length us, event | category | flops | bytes accessed | tf_op | source)
XLA Modules:
  0.0 771.5 jit_solution(2913814473142485360)
XLA Ops:
  1.9 0.8 compare_select_fusion.1
  3.1 65.3 %gather_fusion = s32[16384]{0:T(1024)S(1)} fusion(s32[1024]{0:T(1024)S(1)} %copy-done.1, s32[16384]{0:T(1024)S(1)} %broadcast_clamp_fusion), kind=kCustom, calls=%fused_computation | custom fusion | bytes 196608 | tf_op jit(solution)/shard_map/gather | solution.py:34
  70.4 60.8 %scatter_custom_fusion = s32[262144]{0:T(1024)S(1)} fusion(s32[16384]{0:T(1024)S(1)} %reshape.167, s32[16384]{0:T(1024)} %broadcast.186, s32[]{:T(128)} %constant.52.clone.1), kind=kCustom, calls=%fused_computation.28 | custom fusion | bytes 1049088
  131.2 1.1 reshape.134
  132.3 1.0 constant_dynamic-slice_fusion
  133.4 0.7 reduce_window_sum.22
  134.1 12.3 %all_gather.6 = bf16[16,128,128]{2,1,0:T(8,128)(2,1)S(1)} all-gather(bf16[4,128,128]{2,1,0:T(8,128)(2,1)S(1)} %convert_element_type.38), channel_id=1, replica_groups=mesh['pairs'=64,'orb'=4] {'orb'}, dimensions={0}, use_global_device_ids=true | all-gather | bytes 655360 | tf_op jit(solution)/shard_map/all_gather | solution.py:61
  146.4 0.7 convert_bitcast_fusion.1
  147.1 2.6 copy.45
  149.8 14.2 %all-to-all-start = ((bf16[64,1,128,128]{3,2,1,0:T(8,128)(2,1)}), bf16[64,1,128,128]{3,2,1,0:T(8,128)(2,1)}, u32[]{:S(2)}, u32[]{:S(2)}) async-start(bf16[64,1,128,128]{3,2,1,0:T(8,128)(2,1)} %copy.45), calls=%async_computation | async-start | bytes 4194304 | tf_op jit(solution)/shard_map/all_to_all | solution.py:66
  164.2 0.8 dynamic-slice_reduce_fusion
  165.4 0.7 gather_fusion.1
  167.4 15.0 %psum.28 = f32[32,128]{1,0:T(8,128)S(1)} all-reduce(f32[32,128]{1,0:T(8,128)S(1)} %convolution_add_fusion.1), channel_id=1, replica_groups=mesh['pairs'=64,'orb'=4] {'orb'}, use_global_device_ids=true, to_apply=%region_3.4 | all-reduce | flops 4096 | bytes 32768 | tf_op jit(solution)/shard_map/psum | solution.py:80
  182.4 263.5 %psum.29 = f32[32,128]{1,0:T(8,128)S(1)} all-reduce(f32[32,128]{1,0:T(8,128)S(1)} %psum.28), channel_id=1, replica_groups=mesh['pairs'=64,'orb'=4] {'pairs'}, use_global_device_ids=true, to_apply=%region_4.5 | all-reduce | flops 4096 | bytes 32768 | tf_op jit(solution)/shard_map/psum | solution.py:80
  446.3 3.7 gather_fusion.2
  450.1 3.8 fusion.64
  453.9 10.1 %all_gather.7 = bf16[16,128,128]{2,1,0:T(8,128)(2,1)S(1)} all-gather(bf16[4,128,128]{2,1,0:T(8,128)(2,1)S(1)} %get-tuple-element.4), channel_id=1, replica_groups=mesh['pairs'=64,'orb'=4] {'orb'}, dimensions={0}, use_global_device_ids=true | all-gather | bytes 655360 | tf_op jit(solution)/shard_map/all_gather | solution.py:61
  464.0 0.7 convert_bitcast_fusion
  464.7 2.6 copy.50
  467.4 13.4 %all-to-all-start.1 = ((bf16[64,1,128,128]{3,2,1,0:T(8,128)(2,1)}), bf16[64,1,128,128]{3,2,1,0:T(8,128)(2,1)}, u32[]{:S(2)}, u32[]{:S(2)}) async-start(bf16[64,1,128,128]{3,2,1,0:T(8,128)(2,1)} %copy.50), calls=%async_computation.1 | async-start | bytes 4194304 | tf_op jit(solution)/shard_map/all_to_all | solution.py:66
  481.9 14.7 %psum.30 = f32[32,128]{1,0:T(8,128)S(1)} all-reduce(f32[32,128]{1,0:T(8,128)S(1)} %convolution_add_fusion), channel_id=1, replica_groups=mesh['pairs'=64,'orb'=4] {'orb'}, use_global_device_ids=true, to_apply=%region_5.6 | all-reduce | flops 4096 | bytes 32768 | tf_op jit(solution)/shard_map/psum | solution.py:80
  496.5 266.3 %psum.31 = f32[32,128]{1,0:T(8,128)S(1)} all-reduce(f32[32,128]{1,0:T(8,128)S(1)} %psum.30), channel_id=1, replica_groups=mesh['pairs'=64,'orb'=4] {'pairs'}, use_global_device_ids=true, to_apply=%region_6.7 | all-reduce | flops 4096 | bytes 32768 | tf_op jit(solution)/shard_map/psum | solution.py:80
  763.2 3.7 gather_fusion.3
  766.9 4.6 fusion.40
  (69 shorter events, 7.2 us)
Async XLA Ops:
  0.6 449.4 %copy-start = (bf16[4,16,128,128]{3,2,1,0:T(8,128)(2,1)S(1)}, bf16[4,16,128,128]{3,2,1,0:T(8,128)(2,1)}, u32[]{:S(2)}) copy-start(bf16[4,16,128,128]{3,2,1,0:T(8,128)(2,1)} %param.12) | copy-start | bytes 6291460
  0.6 2.5 copy-start.1
  68.4 0.7 copy-start.3
  68.4 0.7 copy-start.4
  68.4 0.7 copy-start.6
  68.4 0.7 copy-start.9
  68.4 0.8 copy-start.8
  69.7 64.4 %copy-start.2 = (f32[4,128,128]{2,1,0:T(8,128)S(1)}, f32[4,128,128]{2,1,0:T(8,128)}, u32[]{:S(2)}) copy-start(f32[4,128,128]{2,1,0:T(8,128)} %param.9) | copy-start | bytes 786436
  149.8 296.5 %all-to-all-start = ((bf16[64,1,128,128]{3,2,1,0:T(8,128)(2,1)}), bf16[64,1,128,128]{3,2,1,0:T(8,128)(2,1)}, u32[]{:S(2)}, u32[]{:S(2)}) async-start(bf16[64,1,128,128]{3,2,1,0:T(8,128)(2,1)} %copy.45), calls=%async_computation | async-start | bytes 4194304 | tf_op jit(solution)/shard_map/all_to_all | solution.py:66
  164.0 2.4 copy-start.7
  164.0 2.4 copy-start.5
  446.3 3.8 copy-start.10
  446.3 3.8 copy-start.11
  446.3 3.8 copy-start.12
  467.4 295.8 %all-to-all-start.1 = ((bf16[64,1,128,128]{3,2,1,0:T(8,128)(2,1)}), bf16[64,1,128,128]{3,2,1,0:T(8,128)(2,1)}, u32[]{:S(2)}, u32[]{:S(2)}) async-start(bf16[64,1,128,128]{3,2,1,0:T(8,128)(2,1)} %copy.50), calls=%async_computation.1 | async-start | bytes 4194304 | tf_op jit(solution)/shard_map/all_to_all | solution.py:66
